TPU v7x, 512 devices: a whole 4x4x16 slice. The times are simulated.
512 devices in a mesh: grp: 16 (over x, y), dev: 32 (over z, core).
Axes of the slice: x: 4, y: 4, z: 16, core: 2. Of those that a mesh axis runs over, the one named last changes fastest.
Arguments:
- coords: float32 [3, 65536], P(None, ('grp', 'dev')), may hold values from 0 to 1
- field: float32 [65536, 256], P(('grp', 'dev')), may hold values from -6 to 6
- observed: float32 [65536, 256], P(('grp', 'dev')), may hold values from -9 to 9
- pair_owner: int32 [16, 32], replicated, may hold values from 0 to 31, as said below
- cond_list: int32 [1024, 8], replicated, may hold values from 0 to 1023, as said below
- cond_mask: int32 [1024, 8], replicated, may hold values from 0 to 1, as said below
Outputs:
- field_out: float32 [65536, 256], P(('grp', 'dev'))
- last_grad: float32 [65536, 256], P(('grp', 'dev'))
Inputs may be any that keep to these rules, and one draw needn't show every extreme that they name: `pair_owner`: each row is a permutation of the device indices. `cond_list`: a used slot s < 6 of block b names an earlier block of b's group, a used slot s >= 6 a block of the group before; padded slots hold 0; for every group g and devices p, q of it, the used slots of the blocks stored on device p of group g and of those stored on device p of group g + 1 that name blocks stored on device q of group g name one block at most, and no more than one slot names it; this bound is reached. `cond_mask`: blocks of the first group and early blocks of a group have padded slots.
All inputs are finite; a program needn't handle non-finite values.
Results may differ from a plain program's by a relative error of at most 0.0017.
Values may be sent and summed in bfloat16 or wider, within the bound.
A program may use at most 64 MiB of HBM per device.

v0:
```python
import jax
import jax.numpy as jnp
from jax import lax
from jax.sharding import PartitionSpec as P

NCOND = 8
NSAME = 6
STEPS = 2
HIGH = lax.Precision.HIGHEST
LENGTH_SCALE = 0.35
NUGGET = 0.5
STEP_SIZE = 0.3


def shifted(block, axis, distance):
    devices = range(lax.axis_size(axis))
    route = [(i - distance, i) for i in devices if i - distance in devices]
    return lax.ppermute(block, axis, route)


def kernel_of(first, second):
    dist_sq = jnp.zeros((first.shape[1], second.shape[1]), jnp.float32)
    for coord in range(3):
        diff = first[coord][:, None] - second[coord][None, :]
        dist_sq = dist_sq + diff * diff
    return jnp.exp(-jnp.sqrt(dist_sq) / LENGTH_SCALE)


def factor_block(own_x, cond_x, point_mask):
    kcc = kernel_of(cond_x, cond_x) * point_mask[:, None] * point_mask[None, :]
    kcc = kcc + jnp.diag(NUGGET * point_mask + (1.0 - point_mask))
    kci = kernel_of(cond_x, own_x) * point_mask[:, None]
    count = own_x.shape[1]
    kii = kernel_of(own_x, own_x) + NUGGET * jnp.eye(count, dtype=jnp.float32)
    lower = jnp.linalg.cholesky(kcc)
    whiten = lax.linalg.triangular_solve(lower, kci, left_side=True, lower=True)
    regress = lax.linalg.triangular_solve(
        lower, whiten, left_side=True, lower=True, transpose_a=True
    )
    cond_cov = kii - jnp.dot(whiten.T, whiten, precision=HIGH)
    low_cov = jnp.linalg.cholesky(cond_cov)
    inv_low = lax.linalg.triangular_solve(
        low_cov, jnp.eye(count, dtype=jnp.float32), left_side=True, lower=True
    )
    precision = jnp.dot(inv_low.T, inv_low, precision=HIGH)
    return (regress, precision)


def body(coords, field, observed, pair_owner, cond_list, cond_mask):
    groups = lax.axis_size("grp")
    group_members = lax.axis_size("dev")
    my_group = lax.axis_index("grp")
    my_member = lax.axis_index("dev")
    points = field.shape[0] // 2
    out_cols = field.shape[1]
    cross_covariance = NCOND - NSAME
    member_ids = jnp.arange(group_members, dtype=jnp.int32)
    halves = jnp.arange(2, dtype=jnp.int32)
    inverse_factor = jnp.sum(
        jnp.where(
            pair_owner[:, :, None] == member_ids[None, None, :], member_ids[None, :, None], 0
        ),
        axis=1,
    )
    all_lists = cond_list.reshape(groups, group_members, 2, NCOND)
    all_masks = cond_mask.reshape(groups, group_members, 2, NCOND)
    next_group = jnp.minimum(my_group + 1, groups - 1)
    has_next = (my_group + 1 < groups).astype(jnp.int32)
    owner_here = pair_owner[my_group]
    base_id = my_group * 2 * group_members

    def locate(targets):
        pair_idx = jnp.clip((targets - base_id) // 2, 0, group_members - 1)
        return (owner_here[pair_idx], targets % 2)

    here_lists = all_lists[my_group][inverse_factor[my_group]]
    here_masks = all_masks[my_group][inverse_factor[my_group]]
    next_lists = all_lists[next_group][inverse_factor[next_group]][:, :, NSAME:]
    next_masks = all_masks[next_group][inverse_factor[next_group]][:, :, NSAME:] * has_next
    same_owner, same_half = locate(here_lists[:, :, :NSAME])
    fwd_owner, fwd_half = locate(next_lists)
    same_hit = (here_masks[:, :, :NSAME] * (same_owner == my_member))[..., None] * (
        same_half[..., None] == halves
    )
    fwd_hit = (next_masks * (fwd_owner == my_member))[..., None] * (fwd_half[..., None] == halves)
    selector = (jnp.sum(same_hit, axis=(1, 2)) + jnp.sum(fwd_hit, axis=(1, 2))).astype(jnp.float32)
    select_bf = selector.astype(jnp.bfloat16)
    same_valid = here_masks[my_member][:, :NSAME].reshape(-1).astype(jnp.float32)
    fwd_valid = next_masks[my_member].reshape(-1).astype(jnp.float32)
    req_owner = jnp.concatenate(
        [same_owner[my_member].reshape(-1), fwd_owner[my_member].reshape(-1)]
    )
    req_half = jnp.concatenate([same_half[my_member].reshape(-1), fwd_half[my_member].reshape(-1)])
    req_valid = jnp.concatenate([same_valid, fwd_valid])
    req_row = 2 * req_owner + req_half
    my_mask = here_masks[my_member].astype(jnp.float32)
    onehot_same = (
        (same_owner[my_member].reshape(-1)[:, None] == member_ids[None, :]) * same_valid[:, None]
    ).astype(jnp.bfloat16)
    onehot_fwd = (
        (fwd_owner[my_member].reshape(-1)[:, None] == member_ids[None, :]) * fwd_valid[:, None]
    ).astype(jnp.bfloat16)
    own_x = coords.reshape(3, 2, points).transpose(1, 0, 2)
    send_x = (
        selector[:, 0, None, None] * own_x[0][None] + selector[:, 1, None, None] * own_x[1][None]
    )
    recv_x = lax.all_to_all(send_x, "dev", split_axis=0, concat_axis=0, tiled=True)
    got_x = recv_x[req_owner]
    same_x = got_x[: 2 * NSAME].reshape(2, NSAME, 3, points)
    lift_x = shifted(got_x[2 * NSAME :].reshape(2, cross_covariance, 3, points), "grp", 1)
    cond_x = (
        jnp.concatenate([same_x, lift_x], axis=1)
        .transpose(0, 2, 1, 3)
        .reshape(2, 3, NCOND * points)
    )
    point_mask = jnp.repeat(my_mask, points, axis=1)
    regress, precision = jax.vmap(factor_block)(own_x, cond_x, point_mask)
    state = field.reshape(2, points, out_cols)
    target = observed.reshape(2, points, out_cols)
    slot_mask = my_mask[:, :, None, None]
    grad = jnp.zeros_like(state)
    for step_idx in range(STEPS):
        rounded = state.astype(jnp.bfloat16)
        piece = lax.all_gather(rounded, "dev", axis=0, tiled=True)
        rows = jnp.arange(piece.shape[0], dtype=jnp.int32)
        hit = ((req_row[:, None] == rows[None, :]) * req_valid[:, None]).astype(jnp.bfloat16)
        got = jnp.einsum("rn,npo->rpo", hit, piece, preferred_element_type=jnp.float32).astype(
            jnp.bfloat16
        )
        same = got[: 2 * NSAME].reshape(2, NSAME, points, out_cols)
        lifted = shifted(got[2 * NSAME :].reshape(2, cross_covariance, points, out_cols), "grp", 1)
        cond = jnp.concatenate([same, lifted], axis=1).astype(jnp.float32) * slot_mask
        cond = cond.reshape(2, NCOND * points, out_cols)
        resid = state - jnp.einsum("hnp,hno->hpo", regress, cond, precision=HIGH)
        scaled = jnp.einsum("hpq,hqo->hpo", precision, resid, precision=HIGH)
        back = jnp.einsum("hnp,hpo->hno", regress, scaled, precision=HIGH).reshape(
            2, NCOND, points, out_cols
        )
        back = (back * slot_mask).astype(jnp.bfloat16)
        dropped = shifted(back[:, NSAME:], "grp", -1)
        outgo = jnp.einsum(
            "rq,rpo->qpo",
            onehot_same,
            back[:, :NSAME].reshape(2 * NSAME, points, out_cols),
            preferred_element_type=jnp.float32,
        )
        outgo = outgo + jnp.einsum(
            "rq,rpo->qpo",
            onehot_fwd,
            dropped.reshape(2 * cross_covariance, points, out_cols),
            preferred_element_type=jnp.float32,
        )
        returned = lax.all_to_all(
            outgo.astype(jnp.bfloat16), "dev", split_axis=0, concat_axis=0, tiled=True
        )
        incoming = jnp.einsum(
            "qh,qpo->hpo", select_bf, returned, preferred_element_type=jnp.float32
        )
        grad = jnp.tanh(target - state) - (scaled - incoming)
        state = state + STEP_SIZE * grad
    return (state.reshape(2 * points, out_cols), grad.reshape(2 * points, out_cols))


def solution(mesh):
    placed = (
        P(None, ("grp", "dev")),
        P(("grp", "dev"), None),
        P(("grp", "dev"), None),
        P(),
        P(),
        P(),
    )
    return jax.shard_map(
        body,
        mesh=mesh,
        in_specs=placed,
        out_specs=(P(("grp", "dev"), None), P(("grp", "dev"), None)),
        check_vma=False,
    )
```

profile of v0, /device:TPU:3, one launch (start us, length us, event | category | flops | bytes accessed | tf_op | source)
XLA Modules:
  0.0 595.0 jit_solution(17836235499688568392)
XLA Ops:
  11.6 2.7 gather_fusion.1
  15.5 1.2 gather_fusion.4
  19.7 15.9 %all-to-all-start = ((f32[32,1,192]{2,1,0:T(1,128)}), f32[32,1,192]{2,1,0:T(1,128)S(1)}, u32[]{:S(2)}, u32[]{:S(2)}) async-start(f32[32,1,192]{2,1,0:T(1,128)} %reshape.479), calls=%async_computation | async-start | bytes 65536 | tf_op jit(solution)/shard_map/all_to_all | solution.py:107
  40.1 7.6 %all-to-all-done = f32[32,1,192]{2,1,0:T(1,128)S(1)} async-done(((f32[32,1,192]{2,1,0:T(1,128)}), f32[32,1,192]{2,1,0:T(1,128)S(1)}, u32[]{:S(2)}, u32[]{:S(2)}) %all-to-all-start) | async-done | bytes 24608 | tf_op jit(solution)/shard_map/all_to_all | solution.py:107
  49.6 3.2 collective-permute-start
  53.5 2.6 collective-permute-done
  56.8 3.4 add_multiply_fusion
  60.3 1.3 copy-done
  61.6 23.6 %custom-call.43 = f32[2,128,128]{2,1,0:T(8,128)S(1)} custom-call(f32[2,128,128]{2,1,0:T(8,128)S(1)} %cholesky.314), custom_call_target="Cholesky" | custom-call | tf_op jit(solution)/shard_map/vmap(jit(cholesky))/cholesky | solution.py:35
  85.5 19.7 %custom-call.44 = f32[2,1,128,128]{2,3,1,0:T(8,128)S(1)} custom-call(f32[2,1,128,128]{3,2,1,0:T(8,128)S(1)} %select_bitcast_fusion.2), custom_call_target="InvertDiagBlocksLowerTriangular" | custom-call | tf_op jit(solution)/shard_map/vmap(jit(cholesky))/cholesky | solution.py:35
  105.2 1.5 constant_dynamic-update-slice_fusion.3
  106.7 1.5 convolution_subtract_fusion
  108.2 23.5 %custom-call.45 = f32[2,128,128]{2,1,0:T(8,128)S(1)} custom-call(f32[2,128,128]{2,1,0:T(8,128)S(1)} %cholesky.318), custom_call_target="Cholesky" | custom-call | tf_op jit(solution)/shard_map/vmap(jit(cholesky))/cholesky | solution.py:35
  131.7 19.9 %custom-call.46 = f32[2,1,128,128]{2,3,1,0:T(8,128)S(1)} custom-call(f32[2,1,128,128]{3,2,1,0:T(8,128)S(1)} %get-tuple-element.39), custom_call_target="InvertDiagBlocksLowerTriangular" | custom-call | tf_op jit(solution)/shard_map/vmap(jit(cholesky))/cholesky | solution.py:35
  152.0 1.6 convolution_subtract_fusion.1
  153.6 23.5 %custom-call.47 = f32[2,128,128]{2,1,0:T(8,128)S(1)} custom-call(f32[2,128,128]{2,1,0:T(8,128)S(1)} %cholesky.323), custom_call_target="Cholesky" | custom-call | tf_op jit(solution)/shard_map/vmap(jit(cholesky))/cholesky | solution.py:35
  177.0 19.7 %custom-call.48 = f32[2,1,128,128]{2,3,1,0:T(8,128)S(1)} custom-call(f32[2,1,128,128]{3,2,1,0:T(8,128)S(1)} %get-tuple-element.37), custom_call_target="InvertDiagBlocksLowerTriangular" | custom-call | tf_op jit(solution)/shard_map/vmap(jit(cholesky))/cholesky | solution.py:35
  197.0 1.5 convolution_subtract_fusion.2
  198.5 23.9 %custom-call.49 = f32[2,128,128]{2,1,0:T(8,128)S(1)} custom-call(f32[2,128,128]{2,1,0:T(8,128)S(1)} %convolution_subtract_fusion.2), custom_call_target="Cholesky" | custom-call | tf_op jit(solution)/shard_map/vmap(jit(cholesky))/cholesky | solution.py:35
  223.0 1.7 select_select_fusion
  224.7 14.2 %while.1 = (s32[]{:T(128)}, f32[2,512,512]{2,1,0:T(8,128)}, s32[4,2]{0,1:T(2,128)S(1)}, f32[4,2,128,128]{3,2,0,1:T(8,128)}, s32[]{:T(128)}) while((s32[]{:T(128)}, f32[2,512,512]{2,1,0:T(8,128)}, s32[4,2]{0,1:T(2,128)S(1)}, f32[4,2,128,128]{3,2,0,1:T(8,128)}, s32[]{:T(128)}) %tuple.51), condition=%wide.while_cond, body=%wide.while_body.sunk | while | flops 2 | bytes 263777 | solution.py:36
  225.4 2.9 bitcast_dynamic-update-slice_fusion.2
  228.9 2.9 bitcast_dynamic-update-slice_fusion.2
  232.5 2.9 bitcast_dynamic-update-slice_fusion.2
  236.1 2.9 bitcast_dynamic-update-slice_fusion.2
  239.0 79.4 %custom-call.50 = f32[2,4,128,128]{2,3,1,0:T(8,128)S(1)} custom-call(f32[2,4,128,128]{3,2,1,0:T(8,128)} %bitcast.203), custom_call_target="InvertDiagBlocksLowerTriangular" | custom-call | tf_op jit(solution)/shard_map/vmap()/triangular_solve | solution.py:36
  318.9 1.3 convolution_subtract_fusion.6
  320.5 1.4 convolution_subtract_fusion.8
  322.1 1.6 convolution_subtract_fusion.10
  324.7 11.7 %custom-call.51 = f32[2,64,64]{2,1,0:T(8,128)S(1)} custom-call(f32[2,64,64]{2,1,0:T(8,128)S(1)} %fusion.79), custom_call_target="Cholesky" | custom-call | tf_op jit(solution)/shard_map/vmap(jit(cholesky))/cholesky | solution.py:41
  336.7 10.0 %custom-call.52 = f32[2,1,64,64]{2,3,1,0:T(8,128)S(1)} custom-call(f32[2,1,64,64]{3,2,1,0:T(8,128)S(1)} %select_bitcast_fusion.3), custom_call_target="InvertDiagBlocksLowerTriangular" | custom-call | tf_op jit(solution)/shard_map/vmap()/triangular_solve | solution.py:42
  347.3 1.2 convolution_subtract_fusion.5
  348.8 1.3 convolution_subtract_fusion.7
  350.5 1.4 convolution_subtract_fusion.9
  352.3 2.8 fusion.4
  355.2 1.9 collective-permute-start.1
  357.6 5.5 collective-permute-done.1
  364.3 1.0 fusion.134
  365.5 1.9 collective-permute-start.2
  368.0 3.2 collective-permute-done.2
  372.4 63.7 %all_to_all.15 = bf16[32,64,256]{2,1,0:T(8,128)(2,1)S(1)} all-to-all(bf16[32,64,256]{2,1,0:T(8,128)(2,1)S(1)} %copy.165), channel_id=1, replica_groups=mesh['grp'=16,'dev'=32] {'dev'}, dimensions={0} | all-to-all | bytes 2097152 | tf_op jit(solution)/shard_map/all_to_all | solution.py:153
  437.5 62.3 %all-gather.5.cloned.1.call-done = bf16[64,64,256]{2,1,0:T(8,128)(2,1)} async-done(((bf16[2,64,256]{2,1,0:T(8,128)(2,1)}), bf16[64,64,256]{2,1,0:T(8,128)(2,1)}) %all-gather.5.cloned.1.call-update) | async-done | bytes 2097168 | tf_op jit(solution)/shard_map/all_gather | solution.py:124
  499.8 2.8 fusion.7
  502.7 3.1 collective-permute-start.3
  506.0 5.5 collective-permute-done.3
  513.9 2.5 collective-permute-start.4
  516.9 2.7 collective-permute-done.4
  520.8 65.8 %all_to_all.16 = bf16[32,64,256]{2,1,0:T(8,128)(2,1)S(1)} all-to-all(bf16[32,64,256]{2,1,0:T(8,128)(2,1)S(1)} %copy.173), channel_id=1, replica_groups=mesh['grp'=16,'dev'=32] {'dev'}, dimensions={0} | all-to-all | bytes 2097152 | tf_op jit(solution)/shard_map/all_to_all | solution.py:153
  (209 shorter events, 34.5 us)
Async XLA Ops:
  15.5 3.2 copy-start.26
  15.5 20.1 %copy-start.1 = (f32[128,256]{1,0:T(8,128)S(1)}, f32[128,256]{1,0:T(8,128)}, u32[]{:S(2)}) copy-start(f32[128,256]{1,0:T(8,128)} %param.7) | copy-start | bytes 393220
  18.7 17.7 %copy-start.14 = (f32[32,2]{0,1:T(2,128)}, f32[32,2]{0,1:T(2,128)S(1)}, u32[]{:S(2)}) copy-start(f32[32,2]{0,1:T(2,128)S(1)} %add_convert_fusion.2) | copy-start | bytes 772
  19.7 28.0 %all-to-all-start = ((f32[32,1,192]{2,1,0:T(1,128)}), f32[32,1,192]{2,1,0:T(1,128)S(1)}, u32[]{:S(2)}, u32[]{:S(2)}) async-start(f32[32,1,192]{2,1,0:T(1,128)} %reshape.479), calls=%async_computation | async-start | bytes 65536 | tf_op jit(solution)/shard_map/all_to_all | solution.py:107
  35.6 316.7 %all-gather.3.cloned.1.call-start = ((), (), s32[]{:S(2)}) async-start(), calls=%async_computation.3 | async-start | bytes 2162688 | tf_op jit(solution)/shard_map/all_gather | solution.py:124
  36.3 463.4 %all-gather.5.cloned.1.call-start = ((), (), s32[]{:S(2)}) async-start(), calls=%async_computation.4 | async-start | bytes 2162688 | tf_op jit(solution)/shard_map/all_gather | solution.py:124
  36.5 2.5 copy-start.12
  38.0 18.2 %copy-start.18 = (s32[12]{0:T(128)}, s32[12]{0:T(128)S(1)}, u32[]{:S(2)}) copy-start(s32[12]{0:T(128)S(1)} %concatenate.79) | copy-start | bytes 148
  38.2 18.1 %copy-start.16 = (s32[4]{0:T(128)}, s32[4]{0:T(128)S(1)}, u32[]{:S(2)}) copy-start(s32[4]{0:T(128)S(1)} %concatenate.80) | copy-start | bytes 52
  39.3 10.3 %copy-start.21 = (bf16[4]{0:T(256)(128)(2,1)}, bf16[4]{0:T(256)(128)(2,1)S(1)}, u32[]{:S(2)}) copy-start(bf16[4]{0:T(256)(128)(2,1)S(1)} %convert_element_type.103) | copy-start | bytes 28
  39.4 10.2 %copy-start.23 = (bf16[12]{0:T(256)(128)(2,1)}, bf16[12]{0:T(256)(128)(2,1)S(1)}, u32[]{:S(2)}) copy-start(bf16[12]{0:T(256)(128)(2,1)S(1)} %convert_element_type.101) | copy-start | bytes 76
  49.6 6.5 %collective-permute-start = (f32[2,2,3,64]{3,1,0,2:T(2,128)S(1)}, f32[2,2,3,64]{3,1,0,2:T(2,128)S(1)}, u32[]{:S(2)}, u32[]{:S(2)}) collective-permute-start(f32[2,2,3,64]{3,1,0,2:T(2,128)S(1)} %copy.141), channel_id=1, source_target_pairs={{0,32},{32,64},{64,96},{96,128},{128,160},{160,192},{192,224},{224... | collective-permute-start | bytes 9224 | tf_op jit(solution)/shard_map/ppermute | solution.py:18
  56.2 0.6 copy-start.6
  56.2 0.6 copy-start.8
  56.2 0.6 copy-start.10
  60.2 1.3 copy-start
  222.9 1.8 copy-start.27
  223.0 95.4 %copy-start.4 = (f32[2,64]{1,0:T(2,128)S(1)}, f32[2,64]{1,0:T(2,128)}, u32[]{:S(2)}) copy-start(f32[2,64]{1,0:T(2,128)} %get-tuple-element.51) | copy-start | bytes 1540
  223.0 95.4 %copy-start.5 = (f32[2,64]{1,0:T(2,128)S(1)}, f32[2,64]{1,0:T(2,128)}, u32[]{:S(2)}) copy-start(f32[2,64]{1,0:T(2,128)} %get-tuple-element.52) | copy-start | bytes 1540
  223.0 95.4 %copy-start.7 = (f32[2,512]{1,0:T(2,128)S(1)}, f32[2,512]{1,0:T(2,128)}, u32[]{:S(2)}) copy-start(f32[2,512]{1,0:T(2,128)} %copy-done.6) | copy-start | bytes 12292
  223.0 95.4 %copy-start.9 = (f32[2,512]{1,0:T(2,128)S(1)}, f32[2,512]{1,0:T(2,128)}, u32[]{:S(2)}) copy-start(f32[2,512]{1,0:T(2,128)} %copy-done.8) | copy-start | bytes 12292
  223.0 95.4 %copy-start.11 = (f32[2,512]{1,0:T(2,128)S(1)}, f32[2,512]{1,0:T(2,128)}, u32[]{:S(2)}) copy-start(f32[2,512]{1,0:T(2,128)} %copy-done.10) | copy-start | bytes 12292
  239.0 97.5 %copy-start.3 = (pred[64,64]{1,0:T(8,128)(4,1)S(1)}, pred[64,64]{1,0:T(8,128)(4,1)}, u32[]{:S(2)}) copy-start(pred[64,64]{1,0:T(8,128)(4,1)} %iota_compare_fusion.7) | copy-start | bytes 12292
  323.8 28.5 %copy-start.20 = (s32[16]{0:T(128)S(1)}, s32[16]{0:T(128)}, u32[]{:S(2)}) copy-start(s32[16]{0:T(128)} %fusion.115) | copy-start | bytes 196
  323.8 28.5 %copy-start.25 = (bf16[16]{0:T(256)(128)(2,1)S(1)}, bf16[16]{0:T(256)(128)(2,1)}, u32[]{:S(2)}) copy-start(bf16[16]{0:T(256)(128)(2,1)} %pad_maximum_fusion.3) | copy-start | bytes 100
  355.2 7.8 %collective-permute-start.1 = (bf16[2,2,64,256]{3,2,1,0:T(8,128)(2,1)S(1)}, bf16[2,2,64,256]{3,2,1,0:T(8,128)(2,1)S(1)}, u32[]{:S(2)}, u32[]{:S(2)}) collective-permute-start(bf16[2,2,64,256]{3,2,1,0:T(8,128)(2,1)S(1)} %bitcast.195), channel_id=1, source_target_pairs={{0,32},{32,64},{64,96},{96,128},{128,160},{160,192},{192,224},{224... | collective-permute-start | bytes 393224 | tf_op jit(solution)/shard_map/ppermute | solution.py:18
  357.6 7.8 %copy-start.13 = (f32[2,8]{1,0:T(2,128)S(1)}, f32[2,8]{1,0:T(2,128)}, u32[]{:S(2)}) copy-start(f32[2,8]{1,0:T(2,128)} %copy-done.12) | copy-start | bytes 196
  364.3 3.2 copy-start.19
  364.3 3.2 copy-start.24
  365.5 5.8 copy-start.17
  365.5 5.8 copy-start.22
  365.5 5.7 collective-permute-start.2
  371.8 64.3 %copy-start.15 = (f32[32,2]{0,1:T(2,128)S(1)}, f32[32,2]{0,1:T(2,128)}, u32[]{:S(2)}) copy-start(f32[32,2]{0,1:T(2,128)} %copy-done.14) | copy-start | bytes 772
  372.4 64.3 %copy-start.2 = (f32[128,256]{1,0:T(8,128)S(1)}, f32[128,256]{1,0:T(8,128)}, u32[]{:S(2)}) copy-start(f32[128,256]{1,0:T(8,128)} %param.8) | copy-start | bytes 393220
  502.7 8.8 %collective-permute-start.3 = (bf16[2,2,64,256]{3,2,1,0:T(8,128)(2,1)S(1)}, bf16[2,2,64,256]{3,2,1,0:T(8,128)(2,1)S(1)}, u32[]{:S(2)}, u32[]{:S(2)}) collective-permute-start(bf16[2,2,64,256]{3,2,1,0:T(8,128)(2,1)S(1)} %bitcast.196), channel_id=1, source_target_pairs={{0,32},{32,64},{64,96},{96,128},{128,160},{160,192},{192,224},{224... | collective-permute-start | bytes 393224 | tf_op jit(solution)/shard_map/ppermute | solution.py:18
  513.9 5.7 collective-permute-start.4
Sparse Core Ops, SparseCore 0:
  39.1 73.2 all-gather.2
  437.6 62.1 all-gather.4
where the time goes:
time: 602 us; the launch traced here: 595 us
  other arithmetic  269 us (45%)
  blocking collectives  129 us (21%)
  waiting for transfers between devices  89.5 us (15%)
  local copies, waits for them, and re-layouts  31.7 us (5%)
  matrix products  31.7 us (5%)
  starting transfers between devices  28.6 us (5%)
  between operations  15.4 us (3%)
    another operation x18, other arithmetic, factor_block(): lower = jnp.linalg.cholesky(kcc)  154 us
    all_to_all x2, blocking collectives, body(): lax.all_to_all(outgo.astype(jnp.bfloat16), 'dev', split_axis=0, concat_ax...  129 us
    another operation x4, other arithmetic, factor_block(): whiten = lax.linalg.triangular_solve(lower, kci, left_side=True, lower=True)  81.8 us
    all_gather x2, waiting for transfers between devices, body(): piece = lax.all_gather(rounded, 'dev', axis=0, tiled=True)  62.4 us
    ppermute x5, waiting for transfers between devices, shifted(): return lax.ppermute(block, axis, route)  19.5 us
    all_to_all x1, starting transfers between devices, body(): lax.all_to_all(send_x, 'dev', split_axis=0, concat_axis=0, tiled=True)  15.9 us
    another operation x12, local copies, waits for them, and re-layouts  14.2 us
    ppermute x5, starting transfers between devices, shifted(): return lax.ppermute(block, axis, route)  12.6 us
  transfers between devices with their start and end apart: 8, of which 7 were waited for; matrix products, arithmetic and copies ran while one was open for 51% of the time, Pallas kernels for 0%

commit v1 on v0

--- a/solution.py
+++ b/solution.py
@@ -121,7 +121,9 @@
     grad = jnp.zeros_like(state)
     for step_idx in range(STEPS):
         rounded = state.astype(jnp.bfloat16)
-        piece = lax.all_gather(rounded, "dev", axis=0, tiled=True)
+        piece = jnp.concatenate(
+            lax.all_to_all(jnp.stack([rounded] * lax.axis_size("dev")), "dev", 0, 0), axis=0
+        )
         rows = jnp.arange(piece.shape[0], dtype=jnp.int32)
         hit = ((req_row[:, None] == rows[None, :]) * req_valid[:, None]).astype(jnp.bfloat16)
         got = jnp.einsum("rn,npo->rpo", hit, piece, preferred_element_type=jnp.float32).astype(

time: 602 us -> 654 us (1.086)
  blocking collectives: 129 us -> 237 us
  waiting for transfers between devices: 89.5 us -> 28.9 us
  local copies, waits for them, and re-layouts: 31.7 us -> 49.2 us
  between operations: 15.4 us -> 2.24 us
    all_to_all x0 -> x1, blocking collectives: none -> 104 us  [body(): lax.all_to_all(jnp.stack([rounded] * lax.axis_size('dev')), 'dev', 0, 0)]
    all_gather x2 -> x0, waiting for transfers between devices: 62.4 us -> none  [body(): piece = lax.all_gather(rounded, 'dev', axis=0, tiled=True)]
    all_to_all x0 -> x2, local copies, waits for them, and re-layouts: none -> 7.55 us  [body(): lax.all_to_all(jnp.stack([rounded] * lax.axis_size('dev')), 'dev', 0, 0)]
    another operation x12 -> x14, local copies, waits for them, and re-layouts: 14.2 us -> 19.6 us
  transfers between devices with their start and end apart: 8 -> 7, of which waited for: 7 -> 6; matrix products, arithmetic and copies ran while one was open for 51% -> 47% of each run, Pallas kernels for 0% -> 0%
where the time goes in v1:
time: 654 us; the launch traced here: 646 us
  other arithmetic  268 us (41%)
  blocking collectives  237 us (36%)
  local copies, waits for them, and re-layouts  49.2 us (8%)
  starting transfers between devices  32.3 us (5%)
  waiting for transfers between devices  28.9 us (4%)
  matrix products  28.6 us (4%)
    another operation x18, other arithmetic, factor_block(): lower = jnp.linalg.cholesky(kcc)  154 us
    all_to_all x2, blocking collectives, body(): lax.all_to_all(outgo.astype(jnp.bfloat16), 'dev', split_axis=0, concat_ax...  133 us
    all_to_all x1, blocking collectives, body(): lax.all_to_all(jnp.stack([rounded] * lax.axis_size('dev')), 'dev', 0, 0)  104 us
    another operation x4, other arithmetic, factor_block(): whiten = lax.linalg.triangular_solve(lower, kci, left_side=True, lower=True)  81.8 us
    ppermute x5, waiting for transfers between devices, shifted(): return lax.ppermute(block, axis, route)  20.7 us
    all_to_all x1, starting transfers between devices, body(): lax.all_to_all(send_x, 'dev', split_axis=0, concat_axis=0, tiled=True)  15.9 us
    another operation x12, local copies, waits for them, and re-layouts  14.5 us
  transfers between devices with their start and end apart: 7, of which 6 were waited for; matrix products, arithmetic and copies ran while one was open for 47% of the time, Pallas kernels for 0%

profile of v1, /device:TPU:3, one launch (start us, length us, event | category | flops | bytes accessed | tf_op | source)
XLA Modules:
  0.0 645.7 jit_solution(3422968465358168883)
XLA Ops:
  5.1 2.7 gather_fusion.1
  13.1 15.9 %all-to-all-start = ((f32[32,1,192]{2,1,0:T(1,128)}), f32[32,1,192]{2,1,0:T(1,128)S(1)}, u32[]{:S(2)}, u32[]{:S(2)}) async-start(f32[32,1,192]{2,1,0:T(1,128)} %reshape.492), calls=%async_computation | async-start | bytes 65536 | tf_op jit(solution)/shard_map/all_to_all | solution.py:107
  32.8 8.3 %all-to-all-done = f32[32,1,192]{2,1,0:T(1,128)S(1)} async-done(((f32[32,1,192]{2,1,0:T(1,128)}), f32[32,1,192]{2,1,0:T(1,128)S(1)}, u32[]{:S(2)}, u32[]{:S(2)}) %all-to-all-start) | async-done | bytes 24608 | tf_op jit(solution)/shard_map/all_to_all | solution.py:107
  41.1 3.2 stack.4
  44.4 5.5 all-to-all-start.1
  51.8 3.2 collective-permute-start
  55.7 3.0 collective-permute-done
  58.8 3.4 add_multiply_fusion
  63.7 23.7 %custom-call.43 = f32[2,128,128]{2,1,0:T(8,128)S(1)} custom-call(f32[2,128,128]{2,1,0:T(8,128)S(1)} %cholesky.314), custom_call_target="Cholesky" | custom-call | tf_op jit(solution)/shard_map/vmap(jit(cholesky))/cholesky | solution.py:35
  87.6 19.7 %custom-call.44 = f32[2,1,128,128]{2,3,1,0:T(8,128)S(1)} custom-call(f32[2,1,128,128]{3,2,1,0:T(8,128)S(1)} %select_bitcast_fusion.2), custom_call_target="InvertDiagBlocksLowerTriangular" | custom-call | tf_op jit(solution)/shard_map/vmap(jit(cholesky))/cholesky | solution.py:35
  107.3 1.5 constant_dynamic-update-slice_fusion.3
  108.8 1.5 convolution_subtract_fusion
  110.3 23.5 %custom-call.45 = f32[2,128,128]{2,1,0:T(8,128)S(1)} custom-call(f32[2,128,128]{2,1,0:T(8,128)S(1)} %cholesky.318), custom_call_target="Cholesky" | custom-call | tf_op jit(solution)/shard_map/vmap(jit(cholesky))/cholesky | solution.py:35
  133.8 20.1 %custom-call.46 = f32[2,1,128,128]{2,3,1,0:T(8,128)S(1)} custom-call(f32[2,1,128,128]{3,2,1,0:T(8,128)S(1)} %get-tuple-element.39), custom_call_target="InvertDiagBlocksLowerTriangular" | custom-call | tf_op jit(solution)/shard_map/vmap(jit(cholesky))/cholesky | solution.py:35
  154.3 1.6 convolution_subtract_fusion.1
  155.9 23.5 %custom-call.47 = f32[2,128,128]{2,1,0:T(8,128)S(1)} custom-call(f32[2,128,128]{2,1,0:T(8,128)S(1)} %cholesky.323), custom_call_target="Cholesky" | custom-call | tf_op jit(solution)/shard_map/vmap(jit(cholesky))/cholesky | solution.py:35
  179.4 19.7 %custom-call.48 = f32[2,1,128,128]{2,3,1,0:T(8,128)S(1)} custom-call(f32[2,1,128,128]{3,2,1,0:T(8,128)S(1)} %get-tuple-element.37), custom_call_target="InvertDiagBlocksLowerTriangular" | custom-call | tf_op jit(solution)/shard_map/vmap(jit(cholesky))/cholesky | solution.py:35
  199.3 1.5 convolution_subtract_fusion.2
  200.8 23.6 %custom-call.49 = f32[2,128,128]{2,1,0:T(8,128)S(1)} custom-call(f32[2,128,128]{2,1,0:T(8,128)S(1)} %convolution_subtract_fusion.2), custom_call_target="Cholesky" | custom-call | tf_op jit(solution)/shard_map/vmap(jit(cholesky))/cholesky | solution.py:35
  225.1 1.8 select_select_fusion
  226.9 14.5 %while.1 = (s32[]{:T(128)}, f32[2,512,512]{2,1,0:T(8,128)}, s32[4,2]{0,1:T(2,128)S(1)}, f32[4,2,128,128]{3,2,0,1:T(8,128)}, s32[]{:T(128)}) while((s32[]{:T(128)}, f32[2,512,512]{2,1,0:T(8,128)}, s32[4,2]{0,1:T(2,128)S(1)}, f32[4,2,128,128]{3,2,0,1:T(8,128)}, s32[]{:T(128)}) %tuple.51), condition=%wide.while_cond, body=%wide.while_body.sunk | while | flops 2 | bytes 263777 | solution.py:36
  227.5 3.0 bitcast_dynamic-update-slice_fusion.2
  231.1 3.0 bitcast_dynamic-update-slice_fusion.2
  234.8 3.0 bitcast_dynamic-update-slice_fusion.2
  238.4 2.9 bitcast_dynamic-update-slice_fusion.2
  241.3 79.4 %custom-call.50 = f32[2,4,128,128]{2,3,1,0:T(8,128)S(1)} custom-call(f32[2,4,128,128]{3,2,1,0:T(8,128)} %bitcast.209), custom_call_target="InvertDiagBlocksLowerTriangular" | custom-call | tf_op jit(solution)/shard_map/vmap()/triangular_solve | solution.py:36
  322.9 1.4 convolution_subtract_fusion.8
  324.5 1.6 convolution_subtract_fusion.10
  327.0 11.7 %custom-call.51 = f32[2,64,64]{2,1,0:T(8,128)S(1)} custom-call(f32[2,64,64]{2,1,0:T(8,128)S(1)} %fusion.69), custom_call_target="Cholesky" | custom-call | tf_op jit(solution)/shard_map/vmap(jit(cholesky))/cholesky | solution.py:41
  339.0 10.0 %custom-call.52 = f32[2,1,64,64]{2,3,1,0:T(8,128)S(1)} custom-call(f32[2,1,64,64]{3,2,1,0:T(8,128)S(1)} %select_bitcast_fusion.3), custom_call_target="InvertDiagBlocksLowerTriangular" | custom-call | tf_op jit(solution)/shard_map/vmap()/triangular_solve | solution.py:42
  352.9 1.4 convolution_subtract_fusion.9
  354.6 3.9 copy.165
  358.6 2.2 reshape.391
  360.8 2.0 convolution_convert_fusion.1
  363.0 1.9 collective-permute-start.1
  365.3 5.5 collective-permute-done.1
  373.3 1.9 collective-permute-start.2
  375.8 3.2 collective-permute-done.2
  380.2 70.9 %all_to_all.25 = bf16[32,64,256]{2,1,0:T(8,128)(2,1)S(1)} all-to-all(bf16[32,64,256]{2,1,0:T(8,128)(2,1)S(1)} %copy.170), channel_id=1, replica_groups=mesh['grp'=16,'dev'=32] {'dev'}, dimensions={0} | all-to-all | bytes 2097152 | tf_op jit(solution)/shard_map/all_to_all | solution.py:155
  451.9 1.9 stack.5
  453.8 104.2 %all_to_all.26 = bf16[32,2,64,256]{3,1,2,0:T(2,128)(2,1)S(1)} all-to-all(bf16[32,2,64,256]{3,1,2,0:T(2,128)(2,1)S(1)} %stack.5), channel_id=1, replica_groups=mesh['grp'=16,'dev'=32] {'dev'}, dimensions={0} | all-to-all | bytes 4194304 | tf_op jit(solution)/shard_map/all_to_all | solution.py:125
  558.0 3.7 copy.174
  561.6 2.7 reshape.397
  565.0 1.9 collective-permute-start.3
  567.0 5.8 collective-permute-done.3
  575.2 1.9 collective-permute-start.4
  577.7 3.2 collective-permute-done.4
  582.1 61.8 %all_to_all.27 = bf16[32,64,256]{2,1,0:T(8,128)(2,1)S(1)} all-to-all(bf16[32,64,256]{2,1,0:T(8,128)(2,1)S(1)} %copy.179), channel_id=1, replica_groups=mesh['grp'=16,'dev'=32] {'dev'}, dimensions={0} | all-to-all | bytes 2097152 | tf_op jit(solution)/shard_map/all_to_all | solution.py:155
  (214 shorter events, 40.6 us)
Async XLA Ops:
  9.0 3.2 copy-start.26
  9.0 23.1 %copy-start.1 = (f32[128,256]{1,0:T(8,128)S(1)}, f32[128,256]{1,0:T(8,128)}, u32[]{:S(2)}) copy-start(f32[128,256]{1,0:T(8,128)} %param.7) | copy-start | bytes 393220
  12.2 17.2 %copy-start.14 = (f32[32,2]{0,1:T(2,128)}, f32[32,2]{0,1:T(2,128)S(1)}, u32[]{:S(2)}) copy-start(f32[32,2]{0,1:T(2,128)S(1)} %add_convert_fusion.2) | copy-start | bytes 772
  13.1 28.0 %all-to-all-start = ((f32[32,1,192]{2,1,0:T(1,128)}), f32[32,1,192]{2,1,0:T(1,128)S(1)}, u32[]{:S(2)}, u32[]{:S(2)}) async-start(f32[32,1,192]{2,1,0:T(1,128)} %reshape.492), calls=%async_computation | async-start | bytes 65536 | tf_op jit(solution)/shard_map/all_to_all | solution.py:107
  29.1 2.5 copy-start.12
  30.7 24.3 %copy-start.18 = (s32[12]{0:T(128)}, s32[12]{0:T(128)S(1)}, u32[]{:S(2)}) copy-start(s32[12]{0:T(128)S(1)} %concatenate.79) | copy-start | bytes 148
  30.8 24.2 %copy-start.16 = (s32[4]{0:T(128)}, s32[4]{0:T(128)S(1)}, u32[]{:S(2)}) copy-start(s32[4]{0:T(128)S(1)} %concatenate.80) | copy-start | bytes 52
  32.0 12.3 %copy-start.21 = (bf16[4]{0:T(256)(128)(2,1)}, bf16[4]{0:T(256)(128)(2,1)S(1)}, u32[]{:S(2)}) copy-start(bf16[4]{0:T(256)(128)(2,1)S(1)} %convert_element_type.105) | copy-start | bytes 28
  32.1 12.3 %copy-start.23 = (bf16[12]{0:T(256)(128)(2,1)}, bf16[12]{0:T(256)(128)(2,1)S(1)}, u32[]{:S(2)}) copy-start(bf16[12]{0:T(256)(128)(2,1)S(1)} %convert_element_type.103) | copy-start | bytes 76
  44.4 310.3 %all-to-all-start.1 = ((bf16[32,2,64,256]{3,1,2,0:T(2,128)(2,1)}), bf16[32,2,64,256]{3,1,2,0:T(2,128)(2,1)}, u32[]{:S(2)}, u32[]{:S(2)}) async-start(bf16[32,2,64,256]{3,1,2,0:T(2,128)(2,1)} %stack.4), calls=%async_computation.1 | async-start | bytes 4194304 | tf_op jit(solution)/shard_map/all_to_all | solution.py:125
  51.8 6.9 %collective-permute-start = (f32[2,2,3,64]{3,1,0,2:T(2,128)S(1)}, f32[2,2,3,64]{3,1,0,2:T(2,128)S(1)}, u32[]{:S(2)}, u32[]{:S(2)}) collective-permute-start(f32[2,2,3,64]{3,1,0,2:T(2,128)S(1)} %copy.145), channel_id=1, source_target_pairs={{0,32},{32,64},{64,96},{96,128},{128,160},{160,192},{192,224},{224... | collective-permute-start | bytes 9224 | tf_op jit(solution)/shard_map/ppermute | solution.py:18
  58.8 4.8 copy-start.6
  58.8 4.8 copy-start.8
  58.8 4.8 copy-start.10
  62.3 1.4 copy-start
  225.0 1.8 copy-start.27
  225.0 95.7 %copy-start.4 = (f32[2,64]{1,0:T(2,128)S(1)}, f32[2,64]{1,0:T(2,128)}, u32[]{:S(2)}) copy-start(f32[2,64]{1,0:T(2,128)} %get-tuple-element.51) | copy-start | bytes 1540
  225.0 95.7 %copy-start.5 = (f32[2,64]{1,0:T(2,128)S(1)}, f32[2,64]{1,0:T(2,128)}, u32[]{:S(2)}) copy-start(f32[2,64]{1,0:T(2,128)} %get-tuple-element.52) | copy-start | bytes 1540
  225.1 95.7 %copy-start.7 = (f32[2,512]{1,0:T(2,128)S(1)}, f32[2,512]{1,0:T(2,128)}, u32[]{:S(2)}) copy-start(f32[2,512]{1,0:T(2,128)} %copy-done.6) | copy-start | bytes 12292
  225.1 95.7 %copy-start.9 = (f32[2,512]{1,0:T(2,128)S(1)}, f32[2,512]{1,0:T(2,128)}, u32[]{:S(2)}) copy-start(f32[2,512]{1,0:T(2,128)} %copy-done.8) | copy-start | bytes 12292
  225.1 95.7 %copy-start.11 = (f32[2,512]{1,0:T(2,128)S(1)}, f32[2,512]{1,0:T(2,128)}, u32[]{:S(2)}) copy-start(f32[2,512]{1,0:T(2,128)} %copy-done.10) | copy-start | bytes 12292
  241.3 97.4 %copy-start.3 = (pred[64,64]{1,0:T(8,128)(4,1)S(1)}, pred[64,64]{1,0:T(8,128)(4,1)}, u32[]{:S(2)}) copy-start(pred[64,64]{1,0:T(8,128)(4,1)} %iota_compare_fusion.7) | copy-start | bytes 12292
  358.5 2.3 copy-start.20
  358.5 2.3 copy-start.25
  363.0 7.8 %collective-permute-start.1 = (bf16[2,2,64,256]{3,2,1,0:T(8,128)(2,1)S(1)}, bf16[2,2,64,256]{3,2,1,0:T(8,128)(2,1)S(1)}, u32[]{:S(2)}, u32[]{:S(2)}) collective-permute-start(bf16[2,2,64,256]{3,2,1,0:T(8,128)(2,1)S(1)} %bitcast.201), channel_id=1, source_target_pairs={{0,32},{32,64},{64,96},{96,128},{128,160},{160,192},{192,224},{224... | collective-permute-start | bytes 393224 | tf_op jit(solution)/shard_map/ppermute | solution.py:18
  365.3 7.7 %copy-start.13 = (f32[2,8]{1,0:T(2,128)S(1)}, f32[2,8]{1,0:T(2,128)}, u32[]{:S(2)}) copy-start(f32[2,8]{1,0:T(2,128)} %copy-done.12) | copy-start | bytes 196
  372.0 3.2 copy-start.19
  372.0 3.2 copy-start.24
  373.2 5.8 copy-start.17
  373.2 5.8 copy-start.22
  373.3 5.7 collective-permute-start.2
  379.6 71.5 %copy-start.15 = (f32[32,2]{0,1:T(2,128)S(1)}, f32[32,2]{0,1:T(2,128)}, u32[]{:S(2)}) copy-start(f32[32,2]{0,1:T(2,128)} %copy-done.14) | copy-start | bytes 772
  380.2 71.6 %copy-start.2 = (f32[128,256]{1,0:T(8,128)S(1)}, f32[128,256]{1,0:T(8,128)}, u32[]{:S(2)}) copy-start(f32[128,256]{1,0:T(8,128)} %param.8) | copy-start | bytes 393220
  565.0 7.8 %collective-permute-start.3 = (bf16[2,2,64,256]{3,2,1,0:T(8,128)(2,1)S(1)}, bf16[2,2,64,256]{3,2,1,0:T(8,128)(2,1)S(1)}, u32[]{:S(2)}, u32[]{:S(2)}) collective-permute-start(bf16[2,2,64,256]{3,2,1,0:T(8,128)(2,1)S(1)} %bitcast.202), channel_id=1, source_target_pairs={{0,32},{32,64},{64,96},{96,128},{128,160},{160,192},{192,224},{224... | collective-permute-start | bytes 393224 | tf_op jit(solution)/shard_map/ppermute | solution.py:18
  575.2 5.7 collective-permute-start.4
